TPU v7x, 512 devices: a whole 4x4x16 slice. The times are simulated.
512 devices in a mesh: sample: 8 (over x, z_hi), ctx: 64 (over z_lo, y, core).
Axes of the slice: x: 4, y: 4, z: 16 (z_hi: 2, z_lo: 8; z = z_hi * 8 + z_lo), core: 2. Of those that a mesh axis runs over, the one named last changes fastest.
Arguments:
- queries: bfloat16 [16, 512, 8192], P('sample', None, 'ctx'), may hold values from -8 to 8
- prompt_key_value: bfloat16 [2, 2048, 1024], P(None, 'ctx', 'sample'), may hold values from -6 to 6
- continuation_key_value: bfloat16 [2, 16, 512, 1024], P(None, 'sample', 'ctx'), may hold values from -6 to 6
- page_owner: int32 [2048], replicated, may hold values from 0 to 16, as said below
- cont_lengths: int32 [16], replicated, may hold values from 2 to 512, as said below
- branch_offsets: int32 [16], replicated, may hold values from 512 to 2048
Outputs:
- attended: bfloat16 [16, 512, 8192], P('sample', None, 'ctx')
Inputs may be any that keep to these rules, and one draw needn't show every extreme that they name: `page_owner`: constant over each aligned page of 16 positions; 0 marks a page seen by every continuation that branches after it, s + 1 a page seen only by continuation s; some page belongs to continuation 16 - 1. `cont_lengths`: some continuation has all 512 positions live.
All inputs are finite; a program needn't handle non-finite values.
Results may differ from a plain program's by a relative error of at most 0.0045.
Values may be sent and summed in bfloat16 or wider, within the bound.
No kernel may reach another device: no remote copies, remote signals or barrier semaphores. Data moves between devices by JAX's collectives and lax.ppermute only.
A program may use at most 64 MiB of HBM per device.

v0:
```python
import jax
import jax.numpy as jnp
from jax import lax
from jax.sharding import PartitionSpec as P

QUERY_HEADS = 64
KEY_VALUE_HEADS = 8
HEAD_SIZE = 128
neg_large = -1e30
key_block = 256


def attend_part(running, grouped, keys_part, values_part, visible):
    largest, weight_sum, summed = running
    scale = grouped.shape[-1] ** (-0.5)
    if keys_part.ndim == 2:
        scores = jnp.einsum("sthd,nd->sthn", grouped, keys_part, preferred_element_type=jnp.float32)
    else:
        scores = jnp.einsum(
            "sthd,snd->sthn", grouped, keys_part, preferred_element_type=jnp.float32
        )
    cover = visible[:, :, None, :]
    scores = jnp.where(cover, scores * scale, neg_large)
    new_max = jnp.maximum(largest, jnp.max(scores, axis=-1))
    weights = jnp.where(cover, jnp.exp(scores - new_max[..., None]), 0.0)
    rescale = jnp.exp(largest - new_max)
    weight_sum = weight_sum * rescale + jnp.sum(weights, axis=-1)
    rounded = weights.astype(jnp.bfloat16)
    if values_part.ndim == 2:
        product = jnp.einsum(
            "sthn,nd->sthd", rounded, values_part, preferred_element_type=jnp.float32
        )
    else:
        product = jnp.einsum(
            "sthn,snd->sthd", rounded, values_part, preferred_element_type=jnp.float32
        )
    summed = summed * rescale[..., None] + product
    return (new_max, weight_sum, summed)


def attend_blocks(running, grouped, keys_all, values_all, visible, key_axis):
    count_keys = keys_all.shape[key_axis]
    for block_begin in range(0, count_keys, key_block):
        block_end = min(block_begin + key_block, count_keys)
        keys_part = lax.slice_in_dim(keys_all, block_begin, block_end, axis=key_axis)
        values_part = lax.slice_in_dim(values_all, block_begin, block_end, axis=key_axis)
        running = attend_part(
            running, grouped, keys_part, values_part, visible[:, :, block_begin:block_end]
        )
    return running


def initial_state(grouped):
    largest = jnp.full(grouped.shape[:3], neg_large, jnp.float32)
    weight_sum = jnp.zeros(grouped.shape[:3], jnp.float32)
    summed = jnp.zeros(grouped.shape, jnp.float32)
    return (largest, weight_sum, summed)


def prompt_step(grouped, page_owner, offsets_here, sample_ids, column_start):

    def fold_prompt(running, portion, first_row):
        count_keys = portion.shape[1]
        picked = lax.dynamic_slice_in_dim(portion, column_start, HEAD_SIZE, 2)
        positions = jnp.arange(count_keys, dtype=jnp.int32)
        allowed = (page_owner[None, :] == 0) | (page_owner[None, :] == sample_ids[:, None] + 1)
        seen = allowed & (positions[None, :] < offsets_here[:, None])
        return attend_blocks(running, grouped, picked[0], picked[1], seen[:, None, :], 0)

    return fold_prompt


def local(
    queries, prompt_key_value, continuation_key_value, page_owner, cont_lengths, branch_offsets
):
    sequence_local, cont_len, width = queries.shape
    heads_here = width // HEAD_SIZE
    query_groups = QUERY_HEADS // KEY_VALUE_HEADS
    context_count = lax.axis_size("ctx")
    copy_count = context_count // KEY_VALUE_HEADS
    kv_head = lax.axis_index("ctx") * heads_here // query_groups
    base_sample = lax.axis_index("sample") * sequence_local
    sample_ids = base_sample + jnp.arange(sequence_local, dtype=jnp.int32)
    offsets_here = lax.dynamic_slice_in_dim(branch_offsets, base_sample, sequence_local)
    lengths_here = lax.dynamic_slice_in_dim(cont_lengths, base_sample, sequence_local)
    query_pos = jnp.arange(cont_len, dtype=jnp.int32)
    grouped = queries.reshape(sequence_local, cont_len, heads_here, HEAD_SIZE)
    full_heads = lax.all_gather(prompt_key_value, "sample", axis=2, tiled=True)
    fold_prompt = prompt_step(grouped, page_owner, offsets_here, sample_ids, kv_head * HEAD_SIZE)
    running = fold_prompt(
        initial_state(grouped), lax.all_gather(full_heads, "ctx", axis=1, tiled=True), jnp.int32(0)
    )
    continuation_block = continuation_key_value.shape[2]
    spread_continuation = jnp.repeat(
        continuation_key_value.reshape(
            2, sequence_local, continuation_block, KEY_VALUE_HEADS, HEAD_SIZE
        ),
        copy_count,
        axis=3,
    )
    own_cont = lax.all_to_all(spread_continuation, "ctx", split_axis=3, concat_axis=2, tiled=True)
    own_cont = own_cont.reshape(2, sequence_local, continuation_block * context_count, HEAD_SIZE)
    causal = query_pos[None, :, None] >= query_pos[None, None, :]
    live_keys = query_pos[None, None, :] < lengths_here[:, None, None]
    visible = causal & live_keys
    running = attend_blocks(running, grouped, own_cont[0], own_cont[1], visible, 1)
    largest, weight_sum, summed = running
    mixed = summed / weight_sum[..., None]
    live_rows = (query_pos[None, :] < lengths_here[:, None])[:, :, None, None]
    mixed = jnp.where(live_rows, mixed, 0.0)
    return mixed.reshape(sequence_local, cont_len, width).astype(jnp.bfloat16)


def solution(mesh):
    in_specs = (
        P("sample", None, "ctx"),
        P(None, "ctx", "sample"),
        P(None, "sample", "ctx", None),
        P(),
        P(),
        P(),
    )
    out_specs = P("sample", None, "ctx")
    return jax.shard_map(local, mesh=mesh, in_specs=in_specs, out_specs=out_specs, check_vma=False)
```

profile of v0, /device:TPU:1, one launch (start us, length us, event | category | flops | bytes accessed | tf_op | source)
XLA Modules:
  0.0 243.9 jit_solution(1014503203489306723)
XLA Ops:
  6.5 0.0 copy-start
  6.5 0.0 all-gather.2.cloned.1.call-start
  6.5 61.0 %all_gather.6 = bf16[2,32,1024]{2,1,0:T(8,128)(2,1)} all-gather(bf16[2,32,128]{2,1,0:T(8,128)(2,1)} %param.7), channel_id=1, replica_groups=mesh['sample'=8,'ctx'=64] {'sample'}, dimensions={2}, use_global_device_ids=true | all-gather | bytes 147456 | tf_op jit(solution)/shard_map/all_gather | solution.py:88
  67.5 0.0 all-gather.2.cloned.1.call-update
  67.5 0.9 copy.25
  68.4 0.9 broadcast_in_dim.196
  69.3 18.3 %all-to-all-start = ((bf16[2,2,8,64,128]{4,2,1,0,3:T(8,128)(2,1)}), bf16[2,2,8,64,128]{4,2,1,0,3:T(8,128)(2,1)S(1)}, u32[]{:S(2)}, u32[]{:S(2)}) async-start(bf16[2,2,8,64,128]{4,2,1,0,3:T(8,128)(2,1)} %bitcast.49), calls=%async_computation | async-start | bytes 1048576 | tf_op jit(solution)/shard_map/all_to_all | solution.py:101
  87.6 0.7 dynamic_slice.9
  88.3 0.7 dynamic_slice.10
  89.1 0.1 iota_compare_fusion
  89.2 0.1 iota_compare_fusion.1
  89.2 0.7 broadcast_compare_fusion
  89.9 0.8 compare_and_fusion
  90.7 0.3 broadcast_and_fusion
  91.1 31.7 %all-to-all-done = bf16[2,2,8,64,128]{4,2,1,0,3:T(8,128)(2,1)S(1)} async-done(((bf16[2,2,8,64,128]{4,2,1,0,3:T(8,128)(2,1)}), bf16[2,2,8,64,128]{4,2,1,0,3:T(8,128)(2,1)S(1)}, u32[]{:S(2)}, u32[]{:S(2)}) %all-to-all-start) | async-done | bytes 524320 | tf_op jit(solution)/shard_map/all_to_all | solution.py:101
  122.8 0.0 copy-done
  122.8 0.4 fusion.119
  123.2 0.4 fusion.120
  123.7 88.4 %all-gather.2.cloned.1.call-done = bf16[2,2048,1024]{2,1,0:T(8,128)(2,1)} async-done(((bf16[2,32,1024]{2,1,0:T(8,128)(2,1)}), bf16[2,2048,1024]{2,1,0:T(8,128)(2,1)}) %all-gather.2.cloned.1.call-update) | async-done | bytes 8388624 | tf_op jit(solution)/shard_map/all_gather | solution.py:91
  212.1 1.2 fusion.128
  213.2 1.2 fusion.121
  214.4 1.2 fusion.122
  215.6 1.2 fusion.123
  216.8 1.2 fusion.124
  217.9 1.2 fusion.125
  219.1 1.2 fusion.126
  220.3 1.2 fusion.127
  221.5 0.5 fusion.52
  222.0 0.7 fusion.48
  222.7 0.5 fusion.54
  223.2 0.5 fusion.32
  223.7 0.4 fusion.44
  224.1 0.4 fusion.40
  224.5 0.4 fusion.36
  225.0 0.1 multiply_add_fusion
  225.1 1.5 fusion.27
  226.5 1.3 fusion.26
  227.9 1.3 fusion.25
  229.2 1.3 fusion.24
  230.5 1.3 fusion.23
  231.8 1.3 fusion.22
  233.2 1.3 fusion.21
  234.5 2.6 %fusion.31 = bf16[2,512,128]{2,1,0:T(8,128)(2,1)} fusion(f32[2,512,128]{2,1,0:T(8,128)S(1)} %fusion.52, f32[2,512,128]{2,1,0:T(8,128)S(1)} %fusion.54, f32[2,512,128]{2,1,0:T(8,128)S(1)} %fusion.21, f32[2,512,256]{1,2,0:T(8,128)S(1)} %get-tuple-element.43, f32[2,512]{1,0:T(2,128)S(1)} %get-tuple-element.19, pred[2,256]{1,0:T(4,128)(4,1)S(1)} %get-tuple-element.29, ...), kind=kOutput, calls=%fused_computation.49 | convolution fusion | flops 68943872 | bytes 2967052 | tf_op jit(solution)/shard_map/sthn,nd->sthd/dot_general | solution.py:30
  (6 shorter events, 0.1 us)
Async XLA Ops:
  6.5 116.3 %copy-start = (bf16[2,512,128]{2,1,0:T(8,128)(2,1)S(1)}, bf16[2,512,128]{2,1,0:T(8,128)(2,1)}, u32[]{:S(2)}) copy-start(bf16[2,512,128]{2,1,0:T(8,128)(2,1)} %param.6) | copy-start | bytes 786436
  6.5 205.5 %all-gather.2.cloned.1.call-start = ((), (), s32[]{:S(2)}) async-start(), calls=%async_computation.1 | async-start | bytes 8519680 | tf_op jit(solution)/shard_map/all_gather | solution.py:91
  69.3 53.4 %all-to-all-start = ((bf16[2,2,8,64,128]{4,2,1,0,3:T(8,128)(2,1)}), bf16[2,2,8,64,128]{4,2,1,0,3:T(8,128)(2,1)S(1)}, u32[]{:S(2)}, u32[]{:S(2)}) async-start(bf16[2,2,8,64,128]{4,2,1,0,3:T(8,128)(2,1)} %bitcast.49), calls=%async_computation | async-start | bytes 1048576 | tf_op jit(solution)/shard_map/all_to_all | solution.py:101
Sparse Core Ops, SparseCore 0:
  67.7 144.3 all-gather.1
where the time goes:
time: 245 us; the launch traced here: 244 us
  waiting for transfers between devices  120 us (49%)
  blocking collectives  61 us (25%)
  matrix products  23.1 us (9%)
  starting transfers between devices  18.3 us (7%)
  between operations  13.6 us (6%)
  other arithmetic  4.54 us (2%)
  local copies, waits for them, and re-layouts  3.33 us (1%)
    all_gather x1, waiting for transfers between devices, local(): lax.all_gather(full_heads, 'ctx', axis=1, tiled=True)  88.4 us
    all_gather x1, blocking collectives, local(): full_heads = lax.all_gather(prompt_key_value, 'sample', axis=2, tiled=True)  61 us
    all_to_all x1, waiting for transfers between devices, local(): lax.all_to_all(spread_continuation, 'ctx', split_axis=3, concat_axis=2, t...  31.7 us
    all_to_all x1, starting transfers between devices, local(): lax.all_to_all(spread_continuation, 'ctx', split_axis=3, concat_axis=2, t...  18.3 us
    dot_general x8, matrix products, attend_part(): jnp.einsum('sthn,nd->sthd', rounded, values_part, preferred_element_type=...  11.9 us
    dot_general x8, matrix products, attend_part(): jnp.einsum('sthd,nd->sthn', grouped, keys_part, preferred_element_type=jn...  9.32 us
  transfers between devices with their start and end apart: 2, of which 2 were waited for; matrix products, arithmetic and copies ran while one was open for 3% of the time, Pallas kernels for 0%

commit v1 on v0

--- a/solution.py
+++ b/solution.py
@@ -88,7 +88,9 @@
     full_heads = lax.all_gather(prompt_key_value, "sample", axis=2, tiled=True)
     fold_prompt = prompt_step(grouped, page_owner, offsets_here, sample_ids, kv_head * HEAD_SIZE)
     running = fold_prompt(
-        initial_state(grouped), lax.all_gather(full_heads, "ctx", axis=1, tiled=True), jnp.int32(0)
+        initial_state(grouped),
+        jnp.concatenate(lax.all_gather(full_heads, "ctx"), axis=1),
+        jnp.int32(0),
     )
     continuation_block = continuation_key_value.shape[2]
     spread_continuation = jnp.repeat(

time: 245 us -> 254 us (1.037)
  local copies, waits for them, and re-layouts: 3.33 us -> 11.8 us
    all_gather x0 -> x1, local copies, waits for them, and re-layouts: none -> 8.46 us  [local(): lax.all_gather(full_heads, 'ctx')]
  transfers between devices with their start and end apart: 2 -> 2, of which waited for: 2 -> 2; matrix products, arithmetic and copies ran while one was open for 3% -> 2% of each run, Pallas kernels for 0% -> 0%
where the time goes in v1:
time: 254 us; the launch traced here: 252 us
  waiting for transfers between devices  120 us (47%)
  blocking collectives  61 us (24%)
  matrix products  23.1 us (9%)
  starting transfers between devices  18.3 us (7%)
  between operations  13.6 us (5%)
  local copies, waits for them, and re-layouts  11.8 us (5%)
  other arithmetic  4.52 us (2%)
    all_gather x1, waiting for transfers between devices, local(): lax.all_gather(full_heads, 'ctx')  88.5 us
    all_gather x1, blocking collectives, local(): full_heads = lax.all_gather(prompt_key_value, 'sample', axis=2, tiled=True)  61 us
    all_to_all x1, waiting for transfers between devices, local(): lax.all_to_all(spread_continuation, 'ctx', split_axis=3, concat_axis=2, t...  31.7 us
    all_to_all x1, starting transfers between devices, local(): lax.all_to_all(spread_continuation, 'ctx', split_axis=3, concat_axis=2, t...  18.3 us
    dot_general x8, matrix products, attend_part(): jnp.einsum('sthn,nd->sthd', rounded, values_part, preferred_element_type=...  11.9 us
    dot_general x8, matrix products, attend_part(): jnp.einsum('sthd,nd->sthn', grouped, keys_part, preferred_element_type=jn...  9.31 us
    all_gather x1, local copies, waits for them, and re-layouts, local(): lax.all_gather(full_heads, 'ctx')  8.46 us
  transfers between devices with their start and end apart: 2, of which 2 were waited for; matrix products, arithmetic and copies ran while one was open for 2% of the time, Pallas kernels for 0%

profile of v1, /device:TPU:1, one launch (start us, length us, event | category | flops | bytes accessed | tf_op | source)
XLA Modules:
  0.0 252.4 jit_solution(7861142537331305650)
XLA Ops:
  6.5 0.0 copy-start
  6.5 0.0 all-gather.3.cloned.1.call-start
  6.5 61.0 %all_gather.9 = bf16[2,32,1024]{2,1,0:T(8,128)(2,1)} all-gather(bf16[2,32,128]{2,1,0:T(8,128)(2,1)} %param.7), channel_id=1, replica_groups=mesh['sample'=8,'ctx'=64] {'sample'}, dimensions={2}, use_global_device_ids=true | all-gather | bytes 147456 | tf_op jit(solution)/shard_map/all_gather | solution.py:88
  67.5 0.0 all-gather.3.cloned.1.call-update
  67.5 0.9 copy.27
  68.4 0.9 broadcast_in_dim.196
  69.3 18.3 %all-to-all-start = ((bf16[2,2,8,64,128]{4,2,1,0,3:T(8,128)(2,1)}), bf16[2,2,8,64,128]{4,2,1,0,3:T(8,128)(2,1)S(1)}, u32[]{:S(2)}, u32[]{:S(2)}) async-start(bf16[2,2,8,64,128]{4,2,1,0,3:T(8,128)(2,1)} %bitcast.52), calls=%async_computation | async-start | bytes 1048576 | tf_op jit(solution)/shard_map/all_to_all | solution.py:103
  87.6 0.7 dynamic_slice.9
  88.3 0.7 dynamic_slice.10
  89.1 0.1 iota_compare_fusion
  89.2 0.1 iota_compare_fusion.1
  89.2 0.7 broadcast_compare_fusion
  89.9 0.8 compare_and_fusion
  90.7 0.3 broadcast_and_fusion
  91.1 31.7 %all-to-all-done = bf16[2,2,8,64,128]{4,2,1,0,3:T(8,128)(2,1)S(1)} async-done(((bf16[2,2,8,64,128]{4,2,1,0,3:T(8,128)(2,1)}), bf16[2,2,8,64,128]{4,2,1,0,3:T(8,128)(2,1)S(1)}, u32[]{:S(2)}, u32[]{:S(2)}) %all-to-all-start) | async-done | bytes 524320 | tf_op jit(solution)/shard_map/all_to_all | solution.py:103
  122.8 0.0 copy-done
  122.8 0.4 fusion.119
  123.3 0.4 fusion.120
  123.7 88.5 %all-gather.3.cloned.1.call-done = bf16[128,32,1024]{2,1,0:T(8,128)(2,1)} async-done(((bf16[2,32,1024]{2,1,0:T(8,128)(2,1)}), bf16[128,32,1024]{2,1,0:T(8,128)(2,1)}) %all-gather.3.cloned.1.call-update) | async-done | bytes 8388624 | tf_op jit(solution)/shard_map/all_gather | solution.py:92
  212.2 8.5 %copy.18 = bf16[64,2,32,1024]{3,2,0,1:T(8,128)(2,1)} copy(bf16[64,2,32,1024]{3,2,1,0:T(8,128)(2,1)} %bitcast.169) | data formatting | bytes 16777216 | tf_op jit(solution)/shard_map/all_gather | solution.py:92
  220.6 1.2 fusion.128
  221.8 1.2 fusion.121
  223.0 1.2 fusion.122
  224.2 1.2 fusion.123
  225.3 1.2 fusion.124
  226.5 1.2 fusion.125
  227.7 1.2 fusion.126
  228.8 1.2 fusion.127
  230.0 0.5 fusion.52
  230.5 0.7 fusion.48
  231.2 0.5 fusion.54
  231.8 0.4 fusion.32
  232.2 0.4 fusion.44
  232.7 0.4 fusion.40
  233.1 0.4 fusion.36
  233.5 0.1 multiply_add_fusion
  233.6 1.5 fusion.27
  235.1 1.3 fusion.26
  236.4 1.3 fusion.25
  237.7 1.3 fusion.24
  239.1 1.3 fusion.23
  240.4 1.3 fusion.22
  241.7 1.3 fusion.21
  243.0 2.6 %fusion.31 = bf16[2,512,128]{2,1,0:T(8,128)(2,1)} fusion(f32[2,512,128]{2,1,0:T(8,128)S(1)} %fusion.52, f32[2,512,128]{2,1,0:T(8,128)S(1)} %fusion.54, f32[2,512,128]{2,1,0:T(8,128)S(1)} %fusion.21, f32[2,512,256]{1,2,0:T(8,128)S(1)} %get-tuple-element.43, f32[2,512]{1,0:T(2,128)S(1)} %get-tuple-element.19, pred[2,256]{1,0:T(4,128)(4,1)S(1)} %get-tuple-element.29, ...), kind=kOutput, calls=%fused_computation.49 | convolution fusion | flops 68943872 | bytes 2967052 | tf_op jit(solution)/shard_map/sthn,nd->sthd/dot_general | solution.py:30
  (6 shorter events, 0.1 us)
Async XLA Ops:
  6.5 116.3 %copy-start = (bf16[2,512,128]{2,1,0:T(8,128)(2,1)S(1)}, bf16[2,512,128]{2,1,0:T(8,128)(2,1)}, u32[]{:S(2)}) copy-start(bf16[2,512,128]{2,1,0:T(8,128)(2,1)} %param.6) | copy-start | bytes 786436
  6.5 205.7 %all-gather.3.cloned.1.call-start = ((), (), s32[]{:S(2)}) async-start(), calls=%async_computation.1 | async-start | bytes 8519680 | tf_op jit(solution)/shard_map/all_gather | solution.py:92
  69.3 53.4 %all-to-all-start = ((bf16[2,2,8,64,128]{4,2,1,0,3:T(8,128)(2,1)}), bf16[2,2,8,64,128]{4,2,1,0,3:T(8,128)(2,1)S(1)}, u32[]{:S(2)}, u32[]{:S(2)}) async-start(bf16[2,2,8,64,128]{4,2,1,0,3:T(8,128)(2,1)} %bitcast.52), calls=%async_computation | async-start | bytes 1048576 | tf_op jit(solution)/shard_map/all_to_all | solution.py:103
Sparse Core Ops, SparseCore 0:
  67.7 144.4 all-gather.2
